TPU v7x, 512 devices: a whole 4x4x16 slice. The times are simulated.
512 devices in a mesh: row: 64 (over y, z), col: 8 (over x, core).
Axes of the slice: x: 4, y: 4, z: 16, core: 2. Of those that a mesh axis runs over, the one named last changes fastest.
Arguments:
- sketch: bfloat16 [65536, 128], P(('row', 'col')), may hold values from -6 to 6
- degree: float32 [65536], P(('row', 'col')), may hold values from 1 to 64
- block_vals: bfloat16 [64, 8, 16, 128, 128], P('row', 'col'), may hold values from -0.125 to 0.125
- block_rows: int32 [64, 8, 16], P('row', 'col'), may hold values from 0 to 7
- block_cols: int32 [64, 8, 16], P('row', 'col'), may hold values from 0 to 63
- live_count: int32 [64, 8], P('row', 'col'), may hold values from 2 to 16, as said below
Outputs:
- basis: float32 [65536, 128], P(('row', 'col'))
- factor: float32 [128, 128], replicated
Inputs may be any that keep to these rules, and one draw needn't show every extreme that they name: Slots at or past live_count of a device are ignored; some device has all 16 slots live.
All inputs are finite; a program needn't handle non-finite values.
Results may differ from a plain program's by a relative error of at most 0.003.
Values may be sent and summed in bfloat16 or wider, within the bound.
A program may use at most 64 MiB of HBM per device.

v0:
```python
import jax
import jax.numpy as jnp
from jax import lax
from jax.sharding import PartitionSpec as P


def local(sketch, degree, block_vals, block_rows, block_cols, live_count):
    rows_dev = sketch.shape[0]
    rank = sketch.shape[1]
    slots = block_vals.shape[2]
    blk = block_vals.shape[3]
    n_row = lax.axis_size("row")
    n_col = lax.axis_size("col")
    row_blocks = rows_dev * n_col // blk
    col_blocks = rows_dev * n_row // blk
    nodes = rows_dev * n_row * n_col
    values = block_vals.reshape(slots, blk, blk)
    rows_here = block_rows.reshape(slots)
    cols_here = block_cols.reshape(slots)
    live_total = live_count.reshape(())
    slot_ids = lax.iota(jnp.int32, slots)
    block_ids = lax.iota(jnp.int32, row_blocks)
    live = slot_ids < live_total
    table = ((rows_here[:, None] == block_ids[None, :]) & live[:, None]).astype(jnp.float32)
    scale = lax.rsqrt(degree)
    basis = sketch.astype(jnp.float32)
    moved = (scale[:, None] * basis).astype(jnp.bfloat16)
    stripe = lax.all_gather(moved, "row", axis=0, tiled=True)
    stripe_blocks = stripe.reshape(col_blocks, blk, rank)
    picked = jnp.take(stripe_blocks, cols_here, axis=0)
    products = jnp.einsum("nab,nbk->nak", values, picked, preferred_element_type=jnp.float32)
    partial_value = jnp.einsum("nr,nak->rak", table, products, precision=lax.Precision.HIGHEST)
    partial_value = partial_value.reshape(row_blocks * blk, rank)
    summed = lax.psum_scatter(partial_value, "col", scatter_dimension=0, tiled=True)
    image = scale[:, None] * summed
    local_gram = jnp.dot(image.T, image, precision=lax.Precision.HIGHEST)
    gram = lax.psum(local_gram, ("row", "col"))
    gram = gram / nodes
    lower = jnp.linalg.cholesky(gram)
    basis = jax.scipy.linalg.solve_triangular(lower, image.T, lower=True).T
    return (basis, lower.T)


def solution(mesh):
    in_specs = (
        P(("row", "col"), None),
        P(("row", "col")),
        P("row", "col", None, None, None),
        P("row", "col", None),
        P("row", "col", None),
        P("row", "col"),
    )
    out_specs = (P(("row", "col"), None), P())
    return jax.shard_map(local, mesh=mesh, in_specs=in_specs, out_specs=out_specs, check_vma=False)
```

profile of v0, /device:TPU:1, one launch (start us, length us, event | category | flops | bytes accessed | tf_op | source)
XLA Modules:
  0.0 684.9 jit_solution(11248738669199386243)
XLA Ops:
  7.2 0.7 rsqrt.3
  7.9 1.5 multiply_convert_fusion
  9.4 0.0 reduce-scatter.2.cloned.1.call-start
  10.1 0.7 fusion.21
  10.8 0.7 compare_and_fusion
  11.5 136.5 %all-gather.2.cloned.1.call-done = bf16[8192,128]{1,0:T(8,128)(2,1)} async-done(((bf16[128,128]{1,0:T(8,128)(2,1)}), bf16[8192,128]{1,0:T(8,128)(2,1)}) %all-gather.2.cloned.1.call-update) | async-done | bytes 2097168 | tf_op jit(solution)/shard_map/all_gather | solution.py:28
  148.0 2.2 gather_fusion
  150.3 0.7 fusion.2
  151.0 0.5 copy.15
  151.5 0.5 fusion
  152.0 0.9 copy.11
  152.9 0.0 all-reduce.2.cloned.1.call-start
  152.9 43.5 %reduce-scatter.2.cloned.1.call-done = f32[128,128]{1,0:T(8,128)} async-done(((f32[1024,128]{1,0:T(8,128)}), f32[128,128]{1,0:T(8,128)}) %reduce-scatter.2.cloned.1.call-update) | async-done | bytes 65552 | tf_op jit(solution)/shard_map/reduce_scatter | solution.py:34
  196.4 1.9 fusion.11
  198.4 452.9 %all-reduce.2.cloned.1.call-done = f32[128,128]{0,1:T(8,128)} async-done(((f32[128,128]{0,1:T(8,128)}), f32[128,128]{0,1:T(8,128)}) %all-reduce.2.cloned.1.call-update) | async-done | bytes 65552 | tf_op jit(solution)/shard_map/psum | solution.py:37
  651.2 0.8 broadcast_multiply_fusion
  652.1 0.1 copy.13
  652.1 0.9 fusion.9
  653.0 11.7 %cholesky.16 = f32[128,128]{1,0:T(8,128)S(1)} custom-call(f32[128,128]{1,0:T(8,128)S(1)} %fusion.9), custom_call_target="Cholesky" | custom-call | tf_op jit(solution)/shard_map/jit(cholesky)/cholesky | solution.py:39
  664.8 0.6 compare_reduce_fusion
  665.4 0.7 fusion.13
  666.1 9.8 %custom-call.7 = f32[1,128,128]{1,2,0:T(8,128)S(1)} custom-call(f32[1,128,128]{2,1,0:T(8,128)S(1)} %get-tuple-element.7), custom_call_target="InvertDiagBlocksLowerTriangular" | custom-call | tf_op jit(solution)/shard_map/jit(_solve_triangular)/triangular_solve | solution.py:40
  675.9 0.7 copy.14
  676.6 1.7 fusion.7
  (11 shorter events, 0.2 us)
Async XLA Ops:
  7.2 143.1 %copy-start = (bf16[1,1,16,128,128]{4,3,2,1,0:T(8,128)(2,1)S(1)}, bf16[1,1,16,128,128]{4,3,2,1,0:T(8,128)(2,1)}, u32[]{:S(2)}) copy-start(bf16[1,1,16,128,128]{4,3,2,1,0:T(8,128)(2,1)} %param.8) | copy-start | bytes 1572868
  7.2 140.8 %all-gather.2.cloned.1.call-start = ((), (), s32[]{:S(2)}) async-start(), calls=%async_computation.1 | async-start | bytes 2129920 | tf_op jit(solution)/shard_map/all_gather | solution.py:28
  9.4 187.0 %reduce-scatter.2.cloned.1.call-start = ((), (), s32[]{:S(2)}) async-start(), calls=%async_computation.2 | async-start | bytes 589824 | tf_op jit(solution)/shard_map/reduce_scatter | solution.py:34
  150.3 1.2 copy-start.1
  152.9 498.3 %all-reduce.2.cloned.1.call-start = ((), (), s32[]{:S(2)}) async-start(), calls=%async_computation.3 | async-start | bytes 131072 | tf_op jit(solution)/shard_map/psum | solution.py:37
Sparse Core Ops, SparseCore 0:
  11.5 136.4 all-gather.1
  153.0 43.3 reduce-scatter.1
  202.5 448.7 all-reduce.1
where the time goes:
time: 685 us
  waiting for transfers between devices  633 us (92%)
  other arithmetic  27.3 us (4%)
  between operations  14.5 us (2%)
    psum x1, waiting for transfers between devices, local(): gram = lax.psum(local_gram, ('row', 'col'))  453 us
    all_gather x1, waiting for transfers between devices, local(): stripe = lax.all_gather(moved, 'row', axis=0, tiled=True)  137 us
    reduce_scatter x1, waiting for transfers between devices, local(): lax.psum_scatter(partial_value, 'col', scatter_dimension=0, tiled=True)  43.5 us
  transfers between devices with their start and end apart: 3, of which 3 were waited for; matrix products, arithmetic and copies ran while one was open for 0% of the time, Pallas kernels for 0%

commit v1 on v0

--- a/solution.py
+++ b/solution.py
@@ -2,6 +2,7 @@
 import jax.numpy as jnp
 from jax import lax
 from jax.sharding import PartitionSpec as P
+from jax.lax import psum
 
 
 def local(sketch, degree, block_vals, block_rows, block_cols, live_count):
@@ -34,7 +35,12 @@
     summed = lax.psum_scatter(partial_value, "col", scatter_dimension=0, tiled=True)
     image = scale[:, None] * summed
     local_gram = jnp.dot(image.T, image, precision=lax.Precision.HIGHEST)
-    gram = lax.psum(local_gram, ("row", "col"))
+
+    def turn_slabs(mine_x):
+        now = psum(psum(mine_x, "row"), "col")
+        return now
+
+    gram = turn_slabs(local_gram)
     gram = gram / nodes
     lower = jnp.linalg.cholesky(gram)
     basis = jax.scipy.linalg.solve_triangular(lower, image.T, lower=True).T

time: 685 us -> 567 us (0.83)
  waiting for transfers between devices: 633 us -> 514 us
    psum x1 -> x2, waiting for transfers between devices: 453 us -> 334 us  [turn_slabs(): now = psum(psum(mine_x, 'row'), 'col')]
  transfers between devices with their start and end apart: 3 -> 4, of which waited for: 3 -> 4; matrix products, arithmetic and copies ran while one was open for 0% -> 0% of each run, Pallas kernels for 0% -> 0%
where the time goes in v1:
time: 567 us; the launch traced here: 566 us
  waiting for transfers between devices  514 us (91%)
  other arithmetic  27.4 us (5%)
  between operations  14.5 us (3%)
    psum x2, waiting for transfers between devices, turn_slabs(): now = psum(psum(mine_x, 'row'), 'col')  334 us
    all_gather x1, waiting for transfers between devices, local(): stripe = lax.all_gather(moved, 'row', axis=0, tiled=True)  137 us
    reduce_scatter x1, waiting for transfers between devices, local(): lax.psum_scatter(partial_value, 'col', scatter_dimension=0, tiled=True)  43.5 us
    another operation x3, other arithmetic, local(): lower = jnp.linalg.cholesky(gram)  12.4 us
  transfers between devices with their start and end apart: 4, of which 4 were waited for; matrix products, arithmetic and copies ran while one was open for 0% of the time, Pallas kernels for 0%

profile of v1, /device:TPU:1, one launch (start us, length us, event | category | flops | bytes accessed | tf_op | source)
XLA Modules:
  0.0 566.3 jit_solution(10675013685807354658)
XLA Ops:
  7.2 0.7 rsqrt.3
  7.9 1.5 multiply_convert_fusion
  9.4 0.0 reduce-scatter.2.cloned.1.call-start
  10.1 0.7 fusion.21
  10.8 0.7 compare_and_fusion
  11.5 136.5 %all-gather.2.cloned.1.call-done = bf16[8192,128]{1,0:T(8,128)(2,1)} async-done(((bf16[128,128]{1,0:T(8,128)(2,1)}), bf16[8192,128]{1,0:T(8,128)(2,1)}) %all-gather.2.cloned.1.call-update) | async-done | bytes 2097168 | tf_op jit(solution)/shard_map/all_gather | solution.py:29
  148.0 2.2 gather_fusion
  150.3 0.7 fusion.2
  151.0 0.5 copy.15
  151.5 0.5 fusion
  152.0 0.9 copy.11
  152.9 43.5 %reduce-scatter.2.cloned.1.call-done = f32[128,128]{1,0:T(8,128)} async-done(((f32[1024,128]{1,0:T(8,128)}), f32[128,128]{1,0:T(8,128)}) %reduce-scatter.2.cloned.1.call-update) | async-done | bytes 65552 | tf_op jit(solution)/shard_map/reduce_scatter | solution.py:35
  196.4 1.9 fusion.11
  198.4 253.6 %all-reduce.3.cloned.1.call-done = f32[128,128]{0,1:T(8,128)} async-done(((f32[128,128]{0,1:T(8,128)}), f32[128,128]{0,1:T(8,128)}) %all-reduce.3.cloned.1.call-update) | async-done | bytes 65552 | tf_op jit(solution)/shard_map/psum | solution.py:40
  452.1 80.6 %all-reduce.5.cloned.1.call-done = f32[128,128]{0,1:T(8,128)} async-done(((f32[128,128]{0,1:T(8,128)}), f32[128,128]{0,1:T(8,128)}) %all-reduce.5.cloned.1.call-update) | async-done | bytes 65552 | tf_op jit(solution)/shard_map/psum | solution.py:40
  532.7 0.8 broadcast_multiply_fusion
  533.5 0.1 copy.13
  533.6 0.9 fusion.9
  534.5 11.7 %cholesky.16 = f32[128,128]{1,0:T(8,128)S(1)} custom-call(f32[128,128]{1,0:T(8,128)S(1)} %fusion.9), custom_call_target="Cholesky" | custom-call | tf_op jit(solution)/shard_map/jit(cholesky)/cholesky | solution.py:45
  546.2 0.6 compare_reduce_fusion
  546.9 0.7 fusion.13
  547.5 9.8 %custom-call.7 = f32[1,128,128]{1,2,0:T(8,128)S(1)} custom-call(f32[1,128,128]{2,1,0:T(8,128)S(1)} %get-tuple-element.7), custom_call_target="InvertDiagBlocksLowerTriangular" | custom-call | tf_op jit(solution)/shard_map/jit(_solve_triangular)/triangular_solve | solution.py:46
  557.3 0.7 copy.14
  558.1 1.7 fusion.7
  (14 shorter events, 0.3 us)
Async XLA Ops:
  7.2 143.1 %copy-start = (bf16[1,1,16,128,128]{4,3,2,1,0:T(8,128)(2,1)S(1)}, bf16[1,1,16,128,128]{4,3,2,1,0:T(8,128)(2,1)}, u32[]{:S(2)}) copy-start(bf16[1,1,16,128,128]{4,3,2,1,0:T(8,128)(2,1)} %param.8) | copy-start | bytes 1572868
  7.2 140.8 %all-gather.2.cloned.1.call-start = ((), (), s32[]{:S(2)}) async-start(), calls=%async_computation.1 | async-start | bytes 2129920 | tf_op jit(solution)/shard_map/all_gather | solution.py:29
  9.4 187.0 %reduce-scatter.2.cloned.1.call-start = ((), (), s32[]{:S(2)}) async-start(), calls=%async_computation.2 | async-start | bytes 589824 | tf_op jit(solution)/shard_map/reduce_scatter | solution.py:35
  150.3 1.2 copy-start.1
  152.9 299.2 %all-reduce.3.cloned.1.call-start = ((), (), s32[]{:S(2)}) async-start(), calls=%async_computation.3 | async-start | bytes 131072 | tf_op jit(solution)/shard_map/psum | solution.py:40
  198.4 334.3 %all-reduce.5.cloned.1.call-start = ((), (), s32[]{:S(2)}) async-start(), calls=%async_computation.4 | async-start | bytes 131072 | tf_op jit(solution)/shard_map/psum | solution.py:40
Sparse Core Ops, SparseCore 0:
  11.5 136.4 all-gather.1
  153.0 43.3 reduce-scatter.1
  200.4 251.5 all-reduce.2
  454.2 78.4 all-reduce.4

commit v2 on v0

--- a/solution.py
+++ b/solution.py
@@ -1,7 +1,15 @@
+import functools
 import jax
 import jax.numpy as jnp
 from jax import lax
 from jax.sharding import PartitionSpec as P
+
+
+def _get_links(packet, ax_name):
+    return lax.all_gather(packet, ax_name).sum(axis=0)
+
+
+render_skins = functools.partial(_get_links, ax_name=("row", "col"))
 
 
 def local(sketch, degree, block_vals, block_rows, block_cols, live_count):
@@ -34,7 +42,7 @@
     summed = lax.psum_scatter(partial_value, "col", scatter_dimension=0, tiled=True)
     image = scale[:, None] * summed
     local_gram = jnp.dot(image.T, image, precision=lax.Precision.HIGHEST)
-    gram = lax.psum(local_gram, ("row", "col"))
+    gram = render_skins(local_gram)
     gram = gram / nodes
     lower = jnp.linalg.cholesky(gram)
     basis = jax.scipy.linalg.solve_triangular(lower, image.T, lower=True).T

time: 685 us -> 484 us (0.71)
  waiting for transfers between devices: 633 us -> 421 us
  other arithmetic: 27.3 us -> 38.8 us
    psum x1 -> x0, waiting for transfers between devices: 453 us -> none  [local(): gram = lax.psum(local_gram, ('row', 'col'))]
    all_gather x0 -> x1, waiting for transfers between devices: none -> 241 us  [_get_links(): return lax.all_gather(packet, ax_name).sum(axis=0)]
    reduce_sum x0 -> x1, other arithmetic: none -> 13.1 us  [_get_links(): return lax.all_gather(packet, ax_name).sum(axis=0)]
where the time goes in v2:
time: 484 us
  waiting for transfers between devices  421 us (87%)
  other arithmetic  38.8 us (8%)
  between operations  14.5 us (3%)
  local copies, waits for them, and re-layouts  5.16 us (1%)
    all_gather x1, waiting for transfers between devices, _get_links(): return lax.all_gather(packet, ax_name).sum(axis=0)  241 us
    all_gather x1, waiting for transfers between devices, local(): stripe = lax.all_gather(moved, 'row', axis=0, tiled=True)  137 us
    reduce_scatter x1, waiting for transfers between devices, local(): lax.psum_scatter(partial_value, 'col', scatter_dimension=0, tiled=True)  43.5 us
    reduce_sum x1, other arithmetic, _get_links(): return lax.all_gather(packet, ax_name).sum(axis=0)  13.1 us
    another operation x3, other arithmetic, local(): lower = jnp.linalg.cholesky(gram)  12.4 us
    another operation x1, other arithmetic, local(): basis = jax.scipy.linalg.solve_triangular(lower, image.T, lower=True).T  9.81 us
  transfers between devices with their start and end apart: 3, of which 3 were waited for; matrix products, arithmetic and copies ran while one was open for 0% of the time, Pallas kernels for 0%

profile of v2, /device:TPU:1, one launch (start us, length us, event | category | flops | bytes accessed | tf_op | source)
XLA Modules:
  0.0 483.8 jit_solution(17389144522779388520)
XLA Ops:
  7.2 0.0 all-gather.4.cloned.1.call-start
  7.2 0.7 rsqrt.3
  7.9 1.5 multiply_convert_fusion
  9.4 0.0 reduce-scatter.2.cloned.1.call-start
  10.1 0.7 fusion.19
  10.8 0.7 compare_and_fusion
  11.5 136.5 %all-gather.4.cloned.1.call-done = bf16[8192,128]{1,0:T(8,128)(2,1)} async-done(((bf16[128,128]{1,0:T(8,128)(2,1)}), bf16[8192,128]{1,0:T(8,128)(2,1)}) %all-gather.4.cloned.1.call-update) | async-done | bytes 2097168 | tf_op jit(solution)/shard_map/all_gather | solution.py:36
  148.0 2.2 gather_fusion
  150.3 0.7 convolution_bitcast_fusion
  151.0 0.5 copy.18
  151.5 0.5 fusion.15
  152.0 0.9 copy.19
  152.9 0.0 all-gather.6.cloned.1.call-start
  152.9 43.5 %reduce-scatter.2.cloned.1.call-done = f32[128,128]{1,0:T(8,128)} async-done(((f32[1024,128]{1,0:T(8,128)}), f32[128,128]{1,0:T(8,128)}) %reduce-scatter.2.cloned.1.call-update) | async-done | bytes 65552 | tf_op jit(solution)/shard_map/reduce_scatter | solution.py:42
  196.4 1.9 fusion.8
  198.3 241.2 %all-gather.6.cloned.1.call-done = f32[65536,128]{1,0:T(8,128)} async-done(((f32[128,128]{1,0:T(8,128)}), f32[65536,128]{1,0:T(8,128)}) %all-gather.6.cloned.1.call-update) | async-done | bytes 33554448 | tf_op jit(solution)/shard_map/all_gather | solution.py:9
  439.5 13.1 %reduce_sum.11 = f32[128,128]{1,0:T(8,128)S(1)} reduce(f32[512,128,128]{2,1,0:T(8,128)} %bitcast.32, f32[]{:T(128)} %constant.59.clone.1), dimensions={0}, to_apply=%region_1.2 | reduce | flops 8372224 | bytes 33619972 | tf_op jit(solution)/shard_map/reduce_sum | solution.py:9
  452.6 0.1 copy.20
  452.8 11.7 %cholesky.16 = f32[128,128]{1,0:T(8,128)S(1)} custom-call(f32[128,128]{1,0:T(8,128)S(1)} %fusion.6), custom_call_target="Cholesky" | custom-call | tf_op jit(solution)/shard_map/jit(cholesky)/cholesky | solution.py:47
  464.5 0.6 compare_reduce_fusion
  465.1 0.7 fusion.10
  465.8 0.7 copy.21
  466.5 9.8 %custom-call.7 = f32[1,128,128]{1,2,0:T(8,128)S(1)} custom-call(f32[1,128,128]{2,1,0:T(8,128)S(1)} %get-tuple-element.11), custom_call_target="InvertDiagBlocksLowerTriangular" | custom-call | tf_op jit(solution)/shard_map/jit(_solve_triangular)/triangular_solve | solution.py:48
  476.4 0.9 fusion.4
  (13 shorter events, 0.1 us)
Async XLA Ops:
  7.2 143.1 %copy-start = (bf16[1,1,16,128,128]{4,3,2,1,0:T(8,128)(2,1)S(1)}, bf16[1,1,16,128,128]{4,3,2,1,0:T(8,128)(2,1)}, u32[]{:S(2)}) copy-start(bf16[1,1,16,128,128]{4,3,2,1,0:T(8,128)(2,1)} %param.8) | copy-start | bytes 1572868
  7.2 140.8 %all-gather.4.cloned.1.call-start = ((), (), s32[]{:S(2)}) async-start(), calls=%async_computation.1 | async-start | bytes 2129920 | tf_op jit(solution)/shard_map/all_gather | solution.py:36
  9.4 187.0 %reduce-scatter.2.cloned.1.call-start = ((), (), s32[]{:S(2)}) async-start(), calls=%async_computation.2 | async-start | bytes 589824 | tf_op jit(solution)/shard_map/reduce_scatter | solution.py:42
  150.3 1.2 copy-start.2
  152.9 286.6 %all-gather.6.cloned.1.call-start = ((), (), s32[]{:S(2)}) async-start(), calls=%async_computation.3 | async-start | bytes 33619968 | tf_op jit(solution)/shard_map/all_gather | solution.py:9
  439.5 36.8 %copy-start.1 = (f32[128,128]{1,0:T(8,128)S(1)}, f32[128,128]{1,0:T(8,128)}, u32[]{:S(2)}) copy-start(f32[128,128]{1,0:T(8,128)} %reduce-scatter.2.cloned.1.call-done) | copy-start | bytes 196612
Sparse Core Ops, SparseCore 0:
  11.5 136.4 all-gather.3
  153.0 43.3 reduce-scatter.1
  201.5 238.0 all-gather.5
